TPU v7x, 32 devices: a whole 2x2x4 slice. The times are simulated.
32 devices in a mesh: wide: 8 (over z, y), narrow: 4 (over x, core).
Axes of the slice: x: 2, y: 2, z: 4, core: 2. Of those that a mesh axis runs over, the one named last changes fastest.
Arguments:
- frames: bfloat16 [256, 2, 256, 256], P(('wide', 'narrow')), may hold values from -120 to 120
- sketch: bfloat16 [256, 128], replicated, may hold values from -0.3 to 2.3
- kernel_taps: bfloat16 [64], replicated, may hold values from -0.3 to 1.1
Outputs:
- basis: float32 [128, 32768], P(None, ('wide', 'narrow'))
- factor: float32 [128, 128], replicated
All inputs are finite; a program needn't handle non-finite values.
Results may differ from a plain program's by a relative error of at most 0.0043.
Values may be sent and summed in bfloat16 or wider, within the bound.
No kernel may reach another device: no remote copies, remote signals or barrier semaphores. Data moves between devices by JAX's collectives and lax.ppermute only.
A program may use at most 64 MiB of HBM per device.

v0:
```python
import jax
import jax.numpy as jnp
from jax import lax
from jax.sharding import PartitionSpec as P


def gauss_taps(spread):
    position = jnp.arange(15, dtype=jnp.float32) - 7.0
    weights = jnp.exp(-position * position / (2.0 * spread * spread))
    return weights / jnp.sum(weights)


def band_matrix(spread, length):
    outputs = length // 2
    offset_index = (
        jnp.arange(length, dtype=jnp.int32)[None, :]
        - 2 * jnp.arange(outputs, dtype=jnp.int32)[:, None]
        + 7
    )
    weights = gauss_taps(spread)
    matrix = jnp.zeros((outputs, length), jnp.float32)
    for offset in range(15):
        matrix = matrix + jnp.where(offset_index == offset, weights[offset], jnp.float32(0.0))
    return matrix


def filter_volumes(frames_block):
    volume = frames_block.astype(jnp.float32)
    row_count = volume.shape[-2]
    col_count = volume.shape[-1]
    half = col_count // 2
    column_bands = jnp.concatenate(
        [band_matrix(1.5, col_count), band_matrix(3.0, col_count)], axis=0
    )
    column_pass = jnp.einsum(
        "...rc,oc->...ro", volume, column_bands, precision=lax.Precision.HIGHEST
    )
    narrow_pass = jnp.einsum(
        "or,...rc->...oc",
        band_matrix(1.5, row_count),
        column_pass[..., :half],
        precision=lax.Precision.HIGHEST,
    )
    broad_pass = jnp.einsum(
        "or,...rc->...oc",
        band_matrix(3.0, row_count),
        column_pass[..., half:],
        precision=lax.Precision.HIGHEST,
    )
    return (narrow_pass - broad_pass).astype(jnp.bfloat16)


def build_toeplitz(kernel_taps, length):
    lag_index = (
        jnp.arange(length, dtype=jnp.int32)[:, None] - jnp.arange(length, dtype=jnp.int32)[None, :]
    )
    toeplitz = jnp.zeros((length, length), jnp.float32)
    for offset in range(kernel_taps.shape[0]):
        toeplitz = toeplitz + jnp.where(
            lag_index == offset, kernel_taps[offset].astype(jnp.float32), jnp.float32(0.0)
        )
    return toeplitz.astype(jnp.bfloat16)


def high_dot(left, right):
    return jnp.dot(left, right, precision=lax.Precision.HIGHEST, preferred_element_type=jnp.float32)


def shards(frames, sketch, kernel_taps):
    filtered = filter_volumes(frames)
    per_device = frames.shape[0]
    flattened = filtered.reshape(per_device, -1)
    voxel_count = flattened.shape[1]
    group_size = lax.axis_size(("wide", "narrow"))
    block = voxel_count // group_size
    length = per_device * group_size
    toeplitz = build_toeplitz(kernel_taps, length)
    arranged = flattened.reshape(1, per_device, group_size, block)
    received = lax.all_to_all(arranged, ("wide", "narrow"), split_axis=2, concat_axis=0, tiled=True)
    deconvolved = jnp.dot(
        toeplitz, received.reshape(length, received.shape[3]), preferred_element_type=jnp.float32
    ).astype(jnp.bfloat16)
    sketched = lax.dot_general(
        sketch, deconvolved, (((0,), (0,)), ((), ())), preferred_element_type=jnp.float32
    )
    deconvolved, sketched = (deconvolved, sketched)
    series = deconvolved.astype(jnp.float32)
    local_gram = (
        lax.dot_general(
            deconvolved, deconvolved, (((1,), (1,)), ((), ())), preferred_element_type=jnp.float32
        )
        / voxel_count
    )
    data_gram = lax.psum(local_gram, ("wide", "narrow"))
    sketch_full = sketch.astype(jnp.float32)
    weighted = high_dot(data_gram, sketch_full)
    first_lower = jnp.linalg.cholesky(high_dot(sketch_full.T, weighted))
    projected = jax.scipy.linalg.solve_triangular(first_lower, weighted.T, lower=True).T
    second_lower = jnp.linalg.cholesky(high_dot(projected.T, high_dot(data_gram, projected)))
    combined = jax.scipy.linalg.solve_triangular(second_lower, projected.T, lower=True)
    basis = high_dot(combined, series)
    factor = second_lower.T
    return (basis, factor)


def solution(mesh):
    return jax.shard_map(
        shards,
        mesh=mesh,
        in_specs=(P(("wide", "narrow"), None, None, None), P(), P()),
        out_specs=(P(None, ("wide", "narrow")), P()),
        check_vma=False,
    )
```

profile of v0, /device:TPU:0, one launch (start us, length us, event | category | flops | bytes accessed | tf_op | source)
XLA Modules:
  0.0 296.3 jit_solution(4108505157623894362)
XLA Ops:
  7.2 0.0 copy-start
  7.2 0.6 fusion.237
  7.8 0.6 fusion.238
  8.4 0.7 broadcast_divide_fusion.1
  9.1 0.7 fusion.341
  9.8 0.7 broadcast_divide_fusion
  10.4 0.7 fusion.342
  11.1 9.6 %select_add_fusion.1 = f32[128,256]{1,0:T(8,128)S(1)} fusion(f32[]{:T(128)} %bitcast.78, f32[]{:T(128)} %bitcast.77, f32[]{:T(128)} %bitcast.76, f32[]{:T(128)} %bitcast.75, f32[]{:T(128)} %bitcast.74, f32[]{:T(128)} %bitcast.73, f32[]{:T(128)} %bitcast.72, f32[]{:T(128)} %bitcast.71, f32[]{:T(128)} %bitcast.70, f32[]{:T(128)} %bitcast.69, f32[]{:T(128)} %bitcast.68, ...), kind=kLoop, calls=%fused_computation.85 | loop fusion | flops 1507328 | bytes 131644 | tf_op jit(solution)/shard_map/add | solution.py:23
  20.7 9.7 %select_add_fusion = f32[128,256]{1,0:T(8,128)S(1)} fusion(f32[]{:T(128)} %bitcast.93, f32[]{:T(128)} %bitcast.92, f32[]{:T(128)} %bitcast.91, f32[]{:T(128)} %bitcast.90, f32[]{:T(128)} %bitcast.89, f32[]{:T(128)} %bitcast.88, f32[]{:T(128)} %bitcast.87, f32[]{:T(128)} %bitcast.86, f32[]{:T(128)} %bitcast.85, f32[]{:T(128)} %bitcast.84, f32[]{:T(128)} %bitcast.83, ...), kind=kLoop, calls=%fused_computation.84 | loop fusion | flops 1507328 | bytes 131644 | tf_op jit(solution)/shard_map/add | solution.py:23
  30.4 0.0 copy-done
  30.4 1.9 convolution_bitcast_fusion
  32.3 11.5 %fusion = f32[8,2,128,128]{3,2,1,0:T(8,128)S(1)} fusion(f32[8,2,256,256]{2,3,1,0:T(8,128)S(1)} %convolution_bitcast_fusion, f32[]{:T(128)} %bitcast.93, f32[]{:T(128)} %bitcast.92, f32[]{:T(128)} %bitcast.91, f32[]{:T(128)} %bitcast.90, f32[]{:T(128)} %bitcast.89, f32[]{:T(128)} %bitcast.88, f32[]{:T(128)} %bitcast.87, f32[]{:T(128)} %bitcast.86, ...), kind=kOutput, calls=%fused_computation.1 | convolution fusion | flops 806813696 | bytes 3146300 | tf_op jit(solution)/shard_map/or,...rc->...oc/dot_general | solution.py:44
  43.8 11.4 %fusion.10 = bf16[8,2,128,128]{2,3,1,0:T(8,128)(2,1)S(1)} fusion(f32[8,2,128,128]{3,2,1,0:T(8,128)S(1)} %fusion, f32[8,2,256,256]{2,3,1,0:T(8,128)S(1)} %convolution_bitcast_fusion, f32[]{:T(128)} %bitcast.78, f32[]{:T(128)} %bitcast.77, f32[]{:T(128)} %bitcast.76, f32[]{:T(128)} %bitcast.75, f32[]{:T(128)} %bitcast.74, f32[]{:T(128)} %bitcast.73, ...), kind=kOutput, calls=%fused_computation.8 | convolution fusion | flops 807337984 | bytes 3670588 | tf_op jit(solution)/shard_map/or,...rc->...oc/dot_general | solution.py:38
  55.2 0.0 copy-start.1
  55.2 0.3 copy.13
  55.5 0.2 reshape_reshape.3
  55.7 1.1 copy.14
  56.8 7.3 %all-to-all-start = ((bf16[1,8,32,1024]{3,1,0,2:T(8,128)(2,1)}), bf16[1,8,32,1024]{3,1,0,2:T(8,128)(2,1)S(1)}, u32[]{:S(2)}, u32[]{:S(2)}) async-start(bf16[1,8,32,1024]{3,1,0,2:T(8,128)(2,1)} %copy.14), calls=%async_computation | async-start | bytes 1048576 | tf_op jit(solution)/shard_map/all_to_all | solution.py:79
  64.2 0.2 all-reduce.2.cloned.1.call-start
  64.4 0.0 copy-done.1
  64.4 0.7 fusion.338
  70.2 0.7 fusion.337
  83.5 0.7 fusion.339
  102.4 0.7 fusion.340
  107.5 0.0 copy-start.2
  107.5 0.0 all-to-all-done
  107.5 1.1 convolution_convert_fusion
  108.6 1.0 convolution_multiply_fusion
  109.6 0.0 all-reduce.2.cloned.1.call-update
  109.7 128.0 %all-reduce.2.cloned.1.call-done = f32[256,256]{1,0:T(8,128)} async-done(((f32[256,256]{1,0:T(8,128)}), f32[256,256]{1,0:T(8,128)}) %all-reduce.2.cloned.1.call-update) | async-done | bytes 262160 | tf_op jit(solution)/shard_map/psum | solution.py:94
  237.7 0.0 copy-done.2
  237.7 1.2 fusion.343
  238.9 0.3 fusion.344
  239.2 0.1 copy.15
  239.3 11.7 %cholesky.44 = f32[128,128]{1,0:T(8,128)S(1)} custom-call(f32[128,128]{1,0:T(8,128)S(1)} %add_multiply_fusion), custom_call_target="Cholesky" | custom-call | tf_op jit(solution)/shard_map/jit(cholesky)/cholesky | solution.py:97
  251.1 0.6 compare_reduce_fusion.1
  251.7 0.7 fusion.228
  252.4 9.8 %custom-call.6 = f32[1,128,128]{1,2,0:T(8,128)S(1)} custom-call(f32[1,128,128]{2,1,0:T(8,128)S(1)} %fusion.228), custom_call_target="InvertDiagBlocksLowerTriangular" | custom-call | tf_op jit(solution)/shard_map/jit(_solve_triangular)/triangular_solve | solution.py:98
  262.2 0.3 fusion.82
  262.5 1.3 fusion.345
  263.8 0.3 fusion.346
  264.1 0.1 copy.16
  264.2 11.9 %cholesky.55 = f32[128,128]{1,0:T(8,128)S(1)} custom-call(f32[128,128]{1,0:T(8,128)S(1)} %fusion.231), custom_call_target="Cholesky" | custom-call | tf_op jit(solution)/shard_map/jit(cholesky)/cholesky | solution.py:99
  276.1 0.6 compare_reduce_fusion
  276.8 0.7 fusion.236
  277.4 9.8 %custom-call.7 = f32[1,128,128]{1,2,0:T(8,128)S(1)} custom-call(f32[1,128,128]{2,1,0:T(8,128)S(1)} %get-tuple-element.11), custom_call_target="InvertDiagBlocksLowerTriangular" | custom-call | tf_op jit(solution)/shard_map/jit(_solve_triangular)/triangular_solve | solution.py:100
  287.3 0.3 fusion.229
  287.6 1.2 fusion.347
  288.7 0.7 copy.17
  (5 shorter events, 0.1 us)
Async XLA Ops:
  7.2 23.2 %copy-start = (bf16[8,2,256,256]{3,2,1,0:T(8,128)(2,1)S(1)}, bf16[8,2,256,256]{3,2,1,0:T(8,128)(2,1)}, u32[]{:S(2)}) copy-start(bf16[8,2,256,256]{3,2,1,0:T(8,128)(2,1)} %param.6) | copy-start | bytes 6291460
  55.2 9.2 %copy-start.1 = (bf16[64]{0:T(256)(128)(2,1)S(1)}, bf16[64]{0:T(256)(128)(2,1)}, u32[]{:S(2)}) copy-start(bf16[64]{0:T(256)(128)(2,1)} %param.8) | copy-start | bytes 388
  56.8 50.7 %all-to-all-start = ((bf16[1,8,32,1024]{3,1,0,2:T(8,128)(2,1)}), bf16[1,8,32,1024]{3,1,0,2:T(8,128)(2,1)S(1)}, u32[]{:S(2)}, u32[]{:S(2)}) async-start(bf16[1,8,32,1024]{3,1,0,2:T(8,128)(2,1)} %copy.14), calls=%async_computation | async-start | bytes 1048576 | tf_op jit(solution)/shard_map/all_to_all | solution.py:79
  64.2 173.5 %all-reduce.2.cloned.1.call-start = ((), (), s32[]{:S(2)}) async-start(), calls=%async_computation.1 | async-start | bytes 524288 | tf_op jit(solution)/shard_map/psum | solution.py:94
  107.5 130.2 %copy-start.2 = (bf16[256,128]{1,0:T(8,128)(2,1)S(1)}, bf16[256,128]{1,0:T(8,128)(2,1)}, u32[]{:S(2)}) copy-start(bf16[256,128]{1,0:T(8,128)(2,1)} %param.7) | copy-start | bytes 196612
Sparse Core Ops, SparseCore 0:
  109.8 127.8 all-reduce.1
where the time goes:
time: 298 us; the launch traced here: 296 us
  waiting for transfers between devices  128 us (43%)
  other arithmetic  67.7 us (23%)
  between operations  54.4 us (18%)
  matrix products  31.8 us (11%)
  starting transfers between devices  7.54 us (3%)
  local copies, waits for them, and re-layouts  6.83 us (2%)
    psum x1, waiting for transfers between devices, shards(): data_gram = lax.psum(local_gram, ('wide', 'narrow'))  128 us
    add x2, other arithmetic, band_matrix(): matrix + jnp.where(offset_index == offset, weights[offset], jnp.float32(0...  19.2 us
    another operation x3, other arithmetic, shards(): jnp.linalg.cholesky(high_dot(projected.T, high_dot(data_gram, projected)))  12.6 us
    another operation x3, other arithmetic, shards(): first_lower = jnp.linalg.cholesky(high_dot(sketch_full.T, weighted))  12.4 us
    dot_general x1, matrix products, filter_volumes(): jnp.einsum('or,...rc->...oc', band_matrix(3.0, row_count), column_pass[.....  11.5 us
    dot_general x1, matrix products, filter_volumes(): jnp.einsum('or,...rc->...oc', band_matrix(1.5, row_count), column_pass[.....  11.4 us
    another operation x2, other arithmetic, shards(): jax.scipy.linalg.solve_triangular(first_lower, weighted.T, lower=True)  10.5 us
    another operation x1, other arithmetic, shards(): jax.scipy.linalg.solve_triangular(second_lower, projected.T, lower=True)  9.81 us
  transfers between devices with their start and end apart: 2, of which 1 were waited for; matrix products, arithmetic and copies ran while one was open for 1% of the time, Pallas kernels for 0%

commit v1 on v0

--- a/solution.py
+++ b/solution.py
@@ -91,7 +91,8 @@
         )
         / voxel_count
     )
-    data_gram = lax.psum(local_gram, ("wide", "narrow"))
+    state_now = lax.all_gather(local_gram, ("wide", "narrow"))
+    data_gram = jnp.sum(state_now, 0)
     sketch_full = sketch.astype(jnp.float32)
     weighted = high_dot(data_gram, sketch_full)
     first_lower = jnp.linalg.cholesky(high_dot(sketch_full.T, weighted))

time: 298 us -> 250 us (0.84)
  waiting for transfers between devices: 128 us -> 78.4 us
  other arithmetic: 67.7 us -> 71.7 us
    psum x1 -> x0, waiting for transfers between devices: 128 us -> none  [shards(): data_gram = lax.psum(local_gram, ('wide', 'narrow'))]
    all_gather x0 -> x1, waiting for transfers between devices: none -> 78.4 us  [shards(): state_now = lax.all_gather(local_gram, ('wide', 'narrow'))]
    reduce_sum x0 -> x1, other arithmetic: none -> 3.96 us  [shards(): data_gram = jnp.sum(state_now, 0)]
where the time goes in v1:
time: 250 us; the launch traced here: 249 us
  waiting for transfers between devices  78.4 us (31%)
  other arithmetic  71.7 us (29%)
  between operations  54.4 us (22%)
  matrix products  30 us (12%)
  starting transfers between devices  7.55 us (3%)
  local copies, waits for them, and re-layouts  6.8 us (3%)
    all_gather x1, waiting for transfers between devices, shards(): state_now = lax.all_gather(local_gram, ('wide', 'narrow'))  78.4 us
    add x2, other arithmetic, band_matrix(): matrix + jnp.where(offset_index == offset, weights[offset], jnp.float32(0...  19.2 us
    another operation x3, other arithmetic, shards(): jnp.linalg.cholesky(high_dot(projected.T, high_dot(data_gram, projected)))  12.6 us
    another operation x3, other arithmetic, shards(): first_lower = jnp.linalg.cholesky(high_dot(sketch_full.T, weighted))  12.4 us
    dot_general x1, matrix products, filter_volumes(): jnp.einsum('or,...rc->...oc', band_matrix(3.0, row_count), column_pass[.....  11.5 us
    dot_general x1, matrix products, filter_volumes(): jnp.einsum('or,...rc->...oc', band_matrix(1.5, row_count), column_pass[.....  11.4 us
    another operation x2, other arithmetic, shards(): jax.scipy.linalg.solve_triangular(first_lower, weighted.T, lower=True)  10.5 us
    another operation x1, other arithmetic, shards(): jax.scipy.linalg.solve_triangular(second_lower, projected.T, lower=True)  9.81 us
  transfers between devices with their start and end apart: 2, of which 1 were waited for; matrix products, arithmetic and copies ran while one was open for 1% of the time, Pallas kernels for 0%

profile of v1, /device:TPU:0, one launch (start us, length us, event | category | flops | bytes accessed | tf_op | source)
XLA Modules:
  0.0 248.9 jit_solution(8476787075822395015)
XLA Ops:
  7.2 0.0 copy-start
  7.2 0.6 fusion.238
  7.8 0.6 fusion.237
  8.4 0.7 broadcast_divide_fusion.1
  9.1 0.7 broadcast_divide_fusion
  9.7 0.7 fusion.342
  10.5 0.7 fusion.341
  11.2 9.6 %select_add_fusion.1 = f32[128,256]{1,0:T(8,128)S(1)} fusion(f32[]{:T(128)} %bitcast.78, f32[]{:T(128)} %bitcast.77, f32[]{:T(128)} %bitcast.76, f32[]{:T(128)} %bitcast.75, f32[]{:T(128)} %bitcast.74, f32[]{:T(128)} %bitcast.73, f32[]{:T(128)} %bitcast.72, f32[]{:T(128)} %bitcast.71, f32[]{:T(128)} %bitcast.70, f32[]{:T(128)} %bitcast.69, f32[]{:T(128)} %bitcast.68, ...), kind=kLoop, calls=%fused_computation.85 | loop fusion | flops 1507328 | bytes 131644 | tf_op jit(solution)/shard_map/add | solution.py:23
  20.7 9.7 %select_add_fusion = f32[128,256]{1,0:T(8,128)S(1)} fusion(f32[]{:T(128)} %bitcast.93, f32[]{:T(128)} %bitcast.92, f32[]{:T(128)} %bitcast.91, f32[]{:T(128)} %bitcast.90, f32[]{:T(128)} %bitcast.89, f32[]{:T(128)} %bitcast.88, f32[]{:T(128)} %bitcast.87, f32[]{:T(128)} %bitcast.86, f32[]{:T(128)} %bitcast.85, f32[]{:T(128)} %bitcast.84, f32[]{:T(128)} %bitcast.83, ...), kind=kLoop, calls=%fused_computation.84 | loop fusion | flops 1507328 | bytes 131644 | tf_op jit(solution)/shard_map/add | solution.py:23
  30.4 0.0 copy-done
  30.4 2.0 convolution_bitcast_fusion
  32.4 11.5 %fusion = f32[8,2,128,128]{3,2,1,0:T(8,128)S(1)} fusion(f32[8,2,256,256]{2,3,1,0:T(8,128)S(1)} %convolution_bitcast_fusion, f32[]{:T(128)} %bitcast.93, f32[]{:T(128)} %bitcast.92, f32[]{:T(128)} %bitcast.91, f32[]{:T(128)} %bitcast.90, f32[]{:T(128)} %bitcast.89, f32[]{:T(128)} %bitcast.88, f32[]{:T(128)} %bitcast.87, f32[]{:T(128)} %bitcast.86, ...), kind=kOutput, calls=%fused_computation.1 | convolution fusion | flops 806813696 | bytes 3146300 | tf_op jit(solution)/shard_map/or,...rc->...oc/dot_general | solution.py:44
  43.9 11.4 %fusion.10 = bf16[8,2,128,128]{2,3,1,0:T(8,128)(2,1)S(1)} fusion(f32[8,2,128,128]{3,2,1,0:T(8,128)S(1)} %fusion, f32[8,2,256,256]{2,3,1,0:T(8,128)S(1)} %convolution_bitcast_fusion, f32[]{:T(128)} %bitcast.78, f32[]{:T(128)} %bitcast.77, f32[]{:T(128)} %bitcast.76, f32[]{:T(128)} %bitcast.75, f32[]{:T(128)} %bitcast.74, f32[]{:T(128)} %bitcast.73, ...), kind=kOutput, calls=%fused_computation.8 | convolution fusion | flops 807337984 | bytes 3670588 | tf_op jit(solution)/shard_map/or,...rc->...oc/dot_general | solution.py:38
  55.3 0.0 copy-start.1
  55.3 0.3 copy.13
  55.6 0.2 reshape_reshape.3
  55.9 1.1 copy.14
  57.0 7.3 %all-to-all-start = ((bf16[1,8,32,1024]{3,1,0,2:T(8,128)(2,1)}), bf16[1,8,32,1024]{3,1,0,2:T(8,128)(2,1)S(1)}, u32[]{:S(2)}, u32[]{:S(2)}) async-start(bf16[1,8,32,1024]{3,1,0,2:T(8,128)(2,1)} %copy.14), calls=%async_computation | async-start | bytes 1048576 | tf_op jit(solution)/shard_map/all_to_all | solution.py:79
  64.3 0.2 all-gather.3.cloned.1.call-start
  64.5 0.0 copy-done.1
  64.5 0.7 fusion.340
  69.6 0.7 fusion.338
  82.3 0.7 fusion.337
  94.9 0.7 fusion.339
  107.5 0.0 all-to-all-done
  107.5 1.1 convolution_convert_fusion
  108.6 1.0 convolution_multiply_fusion
  109.7 0.0 all-gather.3.cloned.1.call-update
  109.7 78.4 %all-gather.3.cloned.1.call-done = f32[8192,256]{1,0:T(8,128)} async-done(((f32[256,256]{1,0:T(8,128)}), f32[8192,256]{1,0:T(8,128)}) %all-gather.3.cloned.1.call-update) | async-done | bytes 8388624 | tf_op jit(solution)/shard_map/all_gather | solution.py:94
  188.1 0.0 copy-start.2
  188.1 4.0 %reduce_sum.29 = f32[256,256]{1,0:T(8,128)S(1)} reduce(f32[32,256,256]{2,1,0:T(8,128)} %bitcast.223, f32[]{:T(128)} %constant.80.clone.1), dimensions={0}, to_apply=%region_2.3 | reduce | flops 2031616 | bytes 8650756 | tf_op jit(solution)/shard_map/reduce_sum | solution.py:95
  192.1 0.0 copy-done.2
  192.1 0.3 fusion.343
  192.4 0.3 fusion.344
  192.7 0.1 copy.15
  192.8 11.7 %cholesky.44 = f32[128,128]{1,0:T(8,128)S(1)} custom-call(f32[128,128]{1,0:T(8,128)S(1)} %add_multiply_fusion), custom_call_target="Cholesky" | custom-call | tf_op jit(solution)/shard_map/jit(cholesky)/cholesky | solution.py:98
  204.5 0.6 compare_reduce_fusion.1
  205.2 0.7 fusion.228
  205.8 9.8 %custom-call.6 = f32[1,128,128]{1,2,0:T(8,128)S(1)} custom-call(f32[1,128,128]{2,1,0:T(8,128)S(1)} %fusion.228), custom_call_target="InvertDiagBlocksLowerTriangular" | custom-call | tf_op jit(solution)/shard_map/jit(_solve_triangular)/triangular_solve | solution.py:99
  215.7 0.3 fusion.82
  216.0 0.4 fusion.345
  216.4 0.3 fusion.346
  216.6 0.1 copy.16
  216.8 11.9 %cholesky.55 = f32[128,128]{1,0:T(8,128)S(1)} custom-call(f32[128,128]{1,0:T(8,128)S(1)} %fusion.231), custom_call_target="Cholesky" | custom-call | tf_op jit(solution)/shard_map/jit(cholesky)/cholesky | solution.py:100
  228.7 0.6 compare_reduce_fusion
  229.4 0.7 fusion.236
  230.0 0.7 copy.17
  230.8 9.8 %custom-call.7 = f32[1,128,128]{1,2,0:T(8,128)S(1)} custom-call(f32[1,128,128]{2,1,0:T(8,128)S(1)} %get-tuple-element.11), custom_call_target="InvertDiagBlocksLowerTriangular" | custom-call | tf_op jit(solution)/shard_map/jit(_solve_triangular)/triangular_solve | solution.py:101
  240.6 0.3 fusion.229
  240.9 1.2 fusion.347
  (5 shorter events, 0.1 us)
Async XLA Ops:
  7.2 23.2 %copy-start = (bf16[8,2,256,256]{3,2,1,0:T(8,128)(2,1)S(1)}, bf16[8,2,256,256]{3,2,1,0:T(8,128)(2,1)}, u32[]{:S(2)}) copy-start(bf16[8,2,256,256]{3,2,1,0:T(8,128)(2,1)} %param.6) | copy-start | bytes 6291460
  55.3 9.2 %copy-start.1 = (bf16[64]{0:T(256)(128)(2,1)S(1)}, bf16[64]{0:T(256)(128)(2,1)}, u32[]{:S(2)}) copy-start(bf16[64]{0:T(256)(128)(2,1)} %param.8) | copy-start | bytes 388
  57.0 50.6 %all-to-all-start = ((bf16[1,8,32,1024]{3,1,0,2:T(8,128)(2,1)}), bf16[1,8,32,1024]{3,1,0,2:T(8,128)(2,1)S(1)}, u32[]{:S(2)}, u32[]{:S(2)}) async-start(bf16[1,8,32,1024]{3,1,0,2:T(8,128)(2,1)} %copy.14), calls=%async_computation | async-start | bytes 1048576 | tf_op jit(solution)/shard_map/all_to_all | solution.py:79
  64.3 123.8 %all-gather.3.cloned.1.call-start = ((), (), s32[]{:S(2)}) async-start(), calls=%async_computation.1 | async-start | bytes 8650752 | tf_op jit(solution)/shard_map/all_gather | solution.py:94
  188.1 4.0 %copy-start.2 = (bf16[256,128]{1,0:T(8,128)(2,1)S(1)}, bf16[256,128]{1,0:T(8,128)(2,1)}, u32[]{:S(2)}) copy-start(bf16[256,128]{1,0:T(8,128)(2,1)} %param.7) | copy-start | bytes 196612
Sparse Core Ops, SparseCore 0:
  109.8 78.2 all-gather.2
